TPU v7x, 32 devices: a whole 2x2x4 slice. The times are simulated.
32 devices in a mesh: comp: 2 (over core), tile: 16 (over z, y, x).
Axes of the slice: x: 2, y: 2, z: 4, core: 2. Of those that a mesh axis runs over, the one named last changes fastest.
Arguments:
- state: float32 [2, 8, 256, 1024], P('comp', None, 'tile'), may hold values from -80 to 80, as said below
- basis: bfloat16 [12, 2, 8, 256, 1024], P(None, 'comp', None, 'tile'), may hold values from -4 to 4
- kappa: float32 [2, 256, 1024], P('comp', 'tile'), may hold values from 0.05 to 0.22
- vmix: float32 [2, 8, 8], P('comp'), may hold values from -1 to 1
- land_mask: int32 [256, 1024], P('tile'), may hold values 0 or 1
- send_rows: int32 [2, 16, 16, 8], P('comp', 'tile'), may hold values from 0 to 127
- recv_slots: int32 [2, 16, 128, 4], P('comp', 'tile'), may hold values from 0 to 127
- recv_weights: float32 [2, 16, 128, 4], P('comp', 'tile'), may hold values from 0.1 to 0.4
Outputs:
- direction: float32 [2, 8, 256, 1024], P('comp', None, 'tile')
- coefs: float32 [12], replicated
Inputs may be any that keep to these rules, and one draw needn't show every extreme that they name: `state`: the perturbation is noise plus a combination of the basis vectors.
All inputs are finite; a program needn't handle non-finite values. No bound on the sum of `land_mask` on one device may be relied on, other than what follows from the above.
Results may differ from a plain program's by a relative error of at most 0.0003.
Values sent between devices are 32-bit elements; how exact they have to be, the bound alone decides.
No kernel may reach another device: no remote copies, remote signals or barrier semaphores. Data moves between devices by JAX's collectives and lax.ppermute only.
A program may use at most 64 MiB of HBM per device.

v0:
```python
import jax
import jax.numpy as jnp
from jax import lax
from jax.sharding import PartitionSpec as P

FLUX = 4
VECS = 12


def extended(cells, sides, width):
    for axis, dim in sides:
        count = lax.axis_size(axis)
        ends = count - 1
        head = lax.slice_in_dim(cells, 0, width, axis=dim)
        tail = lax.slice_in_dim(cells, cells.shape[dim] - width, cells.shape[dim], axis=dim)
        cells = jnp.concatenate(
            [
                lax.ppermute(tail, axis, [(i, (i + 1) % count) for i in range(ends)]),
                cells,
                lax.ppermute(head, axis, [((i + 1) % count, i) for i in range(ends)]),
            ],
            axis=dim,
        )
    return cells


def from_partner(block, axis, stride):
    count = lax.axis_size(axis)
    route = []
    for low in range(count):
        high = low | 1 << stride
        if high != low and high < count:
            route += [(low, high), (high, low)]
    return lax.ppermute(block, axis, route)


def advance(x, kap, vert_mat, maskf, forced):
    padded = extended(x, (("tile", 1),), 1)
    lap = padded[:, 2:] + padded[:, :-2] + jnp.roll(x, 1, -1) + jnp.roll(x, -1, -1) - 4.0 * x
    vert = jnp.einsum("lm,mrq->lrq", vert_mat, x, precision=lax.Precision.HIGHEST)
    return maskf * (x + kap * lap + vert + forced)


def body(state, basis, kappa, vmix, land_mask, send_rows, recv_slots, recv_weights):
    comp_id = lax.axis_index("comp")
    x = state[0]
    levels, rows, cols = x.shape
    nblk = rows * cols // 128
    surface = x[:FLUX].reshape(FLUX, nblk, 128)
    bucket = surface[:, send_rows[0, 0]]
    moved = lax.all_to_all(bucket, "tile", split_axis=1, concat_axis=1, tiled=True)
    arrived = from_partner(moved, "comp", 0)
    flat = arrived.reshape(FLUX, -1, 128)
    picked = flat[:, recv_slots[0, 0]]
    imported = jnp.einsum(
        "ek,fekq->feq", recv_weights[0, 0], picked, precision=lax.Precision.HIGHEST
    )
    imported = imported.reshape(FLUX, rows, cols)
    forced = jnp.concatenate([imported, jnp.zeros((levels - FLUX, rows, cols), jnp.float32)], 0)
    maskf = jnp.where(comp_id == 0, land_mask.astype(jnp.float32), jnp.float32(1.0))
    for step in range(2):
        x = advance(x, kappa[0], vmix[0], maskf, forced)
    total = float(levels * rows * cols * lax.axis_size("comp") * lax.axis_size("tile"))
    vflat = x.reshape(-1)
    qmat = basis[:, 0].reshape(VECS, -1)
    local_dots = jnp.dot(
        qmat, vflat, precision=lax.Precision.HIGHEST, preferred_element_type=jnp.float32
    )
    local_gram = jnp.dot(qmat, qmat.T, preferred_element_type=jnp.float32)
    dots, squares, gram = lax.psum(
        (local_dots, jnp.sum(vflat * vflat), local_gram), ("comp", "tile")
    )
    coefs = dots / total
    remain = vflat - jnp.dot(
        coefs, qmat, precision=lax.Precision.HIGHEST, preferred_element_type=jnp.float32
    )
    normsq = (
        squares
        - 2.0 * total * jnp.sum(coefs * coefs)
        + jnp.dot(
            coefs,
            jnp.dot(gram, coefs, precision=lax.Precision.HIGHEST),
            precision=lax.Precision.HIGHEST,
        )
    )
    direction = remain / jnp.sqrt(normsq / total + 1e-06)
    return (direction.reshape(1, levels, rows, cols), coefs)


def solution(mesh):
    return jax.shard_map(
        body,
        mesh=mesh,
        in_specs=(
            P("comp", None, "tile", None),
            P(None, "comp", None, "tile", None),
            P("comp", "tile", None),
            P("comp", None, None),
            P("tile", None),
            P("comp", "tile", None, None),
            P("comp", "tile", None, None),
            P("comp", "tile", None, None),
        ),
        out_specs=(P("comp", None, "tile", None), P()),
        check_vma=False,
    )
```

profile of v0, /device:TPU:0, one launch (start us, length us, event | category | flops | bytes accessed | tf_op | source)
XLA Modules:
  0.0 113.7 jit_solution(10225340703240517486)
XLA Ops:
  0.6 0.0 copy-start
  0.6 0.0 copy-start.3
  0.7 1.4 %copy.38 = f32[1,8,16,1024]{3,1,2,0:T(8,128)S(1)} copy(f32[1,8,16,1024]{3,2,1,0:T(8,128)} %param.8) | data formatting | bytes 1048576 | tf_op args[0]
  2.0 1.3 %collective-permute-start = (f32[8,1,1024]{2,0,1:T(8,128)S(1)}, f32[8,1,1024]{2,0,1:T(8,128)S(1)}, u32[]{:S(2)}, u32[]{:S(2)}) collective-permute-start(f32[8,1,1024]{2,0,1:T(8,128)S(1)} %get-tuple-element.17), channel_id=1, source_target_pairs={{1,0},{2,1},{3,2},{4,3},{5,4},{6,5},{7,6},{8,7},{9,8},{10,9},{11,1... | collective-permute-start | bytes 98312 | tf_op jit(solution)/shard_map/ppermute | solution.py:20
  3.3 5.5 %collective-permute-start.1 = (f32[8,1,1024]{2,0,1:T(8,128)S(1)}, f32[8,1,1024]{2,0,1:T(8,128)S(1)}, u32[]{:S(2)}, u32[]{:S(2)}) collective-permute-start(f32[8,1,1024]{2,0,1:T(8,128)S(1)} %get-tuple-element.18), channel_id=1, source_target_pairs={{0,1},{1,2},{2,3},{3,4},{4,5},{5,6},{6,7},{7,8},{8,9},{9,10},{10,1... | collective-permute-start | bytes 98312 | tf_op jit(solution)/shard_map/ppermute | solution.py:18
  8.8 1.0 slice.68
  9.9 0.2 copy.18
  10.0 0.7 compare_select_fusion
  10.7 0.1 copy.17
  10.8 0.1 reshape.90
  10.9 1.4 %gather_fusion = f32[128,4,128]{2,1,0:T(4,128)} fusion(f32[4,128,128]{2,0,1:T(4,128)S(1)} %copy.18, s32[1024]{0:T(1024)S(1)} %pad_clamp_fusion.1), kind=kCustom, calls=%fused_computation | custom fusion | bytes 524800 | tf_op jit(solution)/shard_map/gather | solution.py:50
  12.4 8.2 %all-to-all-start = ((f32[4,16,8,128]{3,0,2,1:T(4,128)}), f32[4,16,8,128]{3,0,2,1:T(4,128)S(1)}, u32[]{:S(2)}, u32[]{:S(2)}) async-start(f32[4,16,8,128]{3,0,2,1:T(4,128)} %bitcast.6), calls=%async_computation | async-start | bytes 524288 | tf_op jit(solution)/shard_map/all_to_all | solution.py:51
  20.5 0.1 fusion.35
  20.6 0.7 compare_select_fusion.1
  21.3 0.1 copy.19
  21.4 0.1 reshape.98
  21.5 0.0 copy-done.3
  21.5 0.1 copy.24
  21.7 2.3 %pad.27 = bf16[16,128,1024]{2,1,0:T(8,128)(2,1)S(1)} pad(bf16[12,128,1024]{2,1,0:T(8,128)(2,1)} %bitcast.89, bf16[]{:T(256)} %constant.53), padding=0_4x0_0x0_0 | pad | bytes 7340034
  24.0 0.0 copy-start.1
  24.0 4.3 %copy.30 = bf16[2,8,128,1024]{3,1,2,0:T(8,128)(2,1)} copy(bf16[2,8,128,1024]{3,2,1,0:T(8,128)(2,1)S(1)} %bitcast.81) | data formatting | bytes 8388608
  28.3 9.4 %fusion.7 = f32[12,12]{1,0:T(8,128)S(1)} fusion(bf16[12,8,16,1024]{3,2,1,0:T(8,128)(2,1)} %bitcast.90), kind=kOutput, calls=%fused_computation.11 | convolution fusion | flops 37748736 | bytes 3146304 | tf_op jit(solution)/shard_map/dot_general | solution.py:69
  37.7 0.0 all-to-all-done
  37.7 0.1 collective-permute-start.2
  37.8 0.2 fusion.34
  38.0 1.3 %collective-permute-done.2 = f32[4,16,8,128]{3,0,2,1:T(4,128)S(1)} collective-permute-done((f32[4,16,8,128]{3,0,2,1:T(4,128)S(1)}, f32[4,16,8,128]{3,0,2,1:T(4,128)S(1)}, u32[]{:S(2)}, u32[]{:S(2)}) %collective-permute-start.2) | collective-permute-done | bytes 262176 | tf_op jit(solution)/shard_map/ppermute | solution.py:34
  39.3 2.3 %gather_fusion.1 = f32[512,4,128]{2,1,0:T(4,128)S(1)} fusion(f32[4,128,128]{2,0,1:T(4,128)S(1)} %bitcast.88, s32[1024]{0:T(1024)S(1)} %pad_clamp_fusion), kind=kCustom, calls=%fused_computation.1 | custom fusion | bytes 2099200 | tf_op jit(solution)/shard_map/gather | solution.py:54
  41.6 2.0 %fusion.11 = f32[128,1,4,128]{3,1,2,0:T(1,128)S(1)} fusion(f32[128,4,1,1]{1,2,3,0:T(1,128)S(1)} %copy.24, f32[4,128,4,128]{3,0,2,1:T(4,128)S(1)} %bitcast.87), kind=kOutput, calls=%fused_computation.15 | convolution fusion | flops 3145728 | bytes 1312768 | tf_op jit(solution)/shard_map/ek,fekq->feq/dot_general | solution.py:55
  43.6 0.0 collective-permute-done
  43.6 0.0 collective-permute-done.1
  43.7 0.9 fusion.6
  44.6 0.2 fusion.31
  44.8 1.3 %collective-permute-start.3 = (f32[8,1,1024]{2,0,1:T(8,128)S(1)}, f32[8,1,1024]{2,0,1:T(8,128)S(1)}, u32[]{:S(2)}, u32[]{:S(2)}) collective-permute-start(f32[8,1,1024]{2,0,1:T(8,128)S(1)} %get-tuple-element.11), channel_id=1, source_target_pairs={{1,0},{2,1},{3,2},{4,3},{5,4},{6,5},{7,6},{8,7},{9,8},{10,9},{11,1... | collective-permute-start | bytes 98312 | tf_op jit(solution)/shard_map/ppermute | solution.py:20
  46.1 4.5 %collective-permute-start.4 = (f32[8,1,1024]{2,0,1:T(8,128)S(1)}, f32[8,1,1024]{2,0,1:T(8,128)S(1)}, u32[]{:S(2)}, u32[]{:S(2)}) collective-permute-start(f32[8,1,1024]{2,0,1:T(8,128)S(1)} %get-tuple-element.12), channel_id=1, source_target_pairs={{0,1},{1,2},{2,3},{3,4},{4,5},{5,6},{6,7},{7,8},{8,9},{9,10},{10,1... | collective-permute-start | bytes 98312 | tf_op jit(solution)/shard_map/ppermute | solution.py:18
  50.6 0.1 fusion.32
  50.7 0.0 collective-permute-done.3
  50.7 1.5 %collective-permute-done.4 = f32[8,1,1024]{2,0,1:T(8,128)S(1)} collective-permute-done((f32[8,1,1024]{2,0,1:T(8,128)S(1)}, f32[8,1,1024]{2,0,1:T(8,128)S(1)}, u32[]{:S(2)}, u32[]{:S(2)}) %collective-permute-start.4) | collective-permute-done | bytes 32800 | tf_op jit(solution)/shard_map/ppermute | solution.py:18
  52.2 1.4 %multiply_reduce_fusion = (f32[]{:T(128)}, f32[8,16,1024]{2,0,1:T(8,128)S(1)}) fusion(f32[4,16,1024]{2,0,1:T(4,128)S(1)} %bitcast.94, f32[8,16,1024]{2,0,1:T(8,128)S(1)} %fusion.6, f32[1,8,8]{2,1,0:T(8,128)S(1)} %copy-done, f32[8,16,1]{2,0,1:T(8,128)S(1)} %get-tuple-element.9, f32[8,16,1023]{2,0,1:T(8,128)S(1)} %get-tuple-element.7, ...), kind=kOutput, calls=%fused_computation.35 | convolution fusion | flops 14680063 | bytes 2556164 | tf_op jit(solution)/shard_map/lm,mrq->lrq/dot_general | solution.py:40
  53.7 0.3 copy.20
  54.0 0.6 reshape.109
  54.6 6.5 %convolution_bitcast_fusion.1 = f32[12]{0:T(128)S(1)} fusion(f32[131072,1]{0,1:T(1,128)S(1)} %reshape.109, bf16[12,131072]{1,0:T(8,128)(2,1)} %bitcast.79), kind=kOutput, calls=%fused_computation.12 | convolution fusion | flops 18874368 | bytes 3670064 | tf_op jit(solution)/shard_map/dot_general | solution.py:66
  61.1 44.3 %all-reduce.1 = (f32[12]{0:T(128)S(1)}, f32[]{:T(128)}, f32[12,12]{1,0:T(8,128)S(1)}) all-reduce(f32[12]{0:T(128)S(1)} %convolution_bitcast_fusion.1, f32[]{:T(128)} %get-tuple-element.19, f32[12,12]{1,0:T(8,128)S(1)} %fusion.7), channel_id=1, replica_groups=mesh['comp'=2,'tile'=16] {'comp','tile'}, use_global_device_ids=true, to_apply=%region_0.1 | all-reduce | flops 157 | bytes 1256 | tf_op jit(solution)/shard_map/psum | solution.py:70
  105.4 0.6 multiply_reduce_fusion.1
  106.0 4.0 %fusion.29 = f32[1,131072]{1,0:T(1,128)S(1)} fusion(bf16[12,131072]{1,0:T(8,128)(2,1)} %bitcast.80, f32[12]{0:T(128)S(1)} %get-tuple-element.6), kind=kOutput, calls=%fused_computation.45 | convolution fusion | flops 18874368 | bytes 3670064 | tf_op jit(solution)/shard_map/dot_general | solution.py:74
  110.0 0.8 fusion.13
  112.7 0.1 copy.29
  112.8 0.1 subtract_divide_fusion
  112.8 0.9 reshape.87
  (12 shorter events, 0.1 us)
Async XLA Ops:
  0.6 43.0 %copy-start = (f32[1,8,8]{2,1,0:T(8,128)S(1)}, f32[1,8,8]{2,1,0:T(8,128)}, u32[]{:S(2)}) copy-start(f32[1,8,8]{2,1,0:T(8,128)} %param.11) | copy-start | bytes 772
  0.6 20.9 %copy-start.3 = (f32[1,1,128,4]{2,3,1,0:T(4,128)S(1)}, f32[1,1,128,4]{2,3,1,0:T(4,128)}, u32[]{:S(2)}) copy-start(f32[1,1,128,4]{2,3,1,0:T(4,128)} %param.15) | copy-start | bytes 6148
  2.0 41.6 %collective-permute-start = (f32[8,1,1024]{2,0,1:T(8,128)S(1)}, f32[8,1,1024]{2,0,1:T(8,128)S(1)}, u32[]{:S(2)}, u32[]{:S(2)}) collective-permute-start(f32[8,1,1024]{2,0,1:T(8,128)S(1)} %get-tuple-element.17), channel_id=1, source_target_pairs={{1,0},{2,1},{3,2},{4,3},{5,4},{6,5},{7,6},{8,7},{9,8},{10,9},{11,1... | collective-permute-start | bytes 98312 | tf_op jit(solution)/shard_map/ppermute | solution.py:20
  3.3 40.3 %collective-permute-start.1 = (f32[8,1,1024]{2,0,1:T(8,128)S(1)}, f32[8,1,1024]{2,0,1:T(8,128)S(1)}, u32[]{:S(2)}, u32[]{:S(2)}) collective-permute-start(f32[8,1,1024]{2,0,1:T(8,128)S(1)} %get-tuple-element.18), channel_id=1, source_target_pairs={{0,1},{1,2},{2,3},{3,4},{4,5},{5,6},{6,7},{7,8},{8,9},{9,10},{10,1... | collective-permute-start | bytes 98312 | tf_op jit(solution)/shard_map/ppermute | solution.py:18
  12.4 25.4 %all-to-all-start = ((f32[4,16,8,128]{3,0,2,1:T(4,128)}), f32[4,16,8,128]{3,0,2,1:T(4,128)S(1)}, u32[]{:S(2)}, u32[]{:S(2)}) async-start(f32[4,16,8,128]{3,0,2,1:T(4,128)} %bitcast.6), calls=%async_computation | async-start | bytes 524288 | tf_op jit(solution)/shard_map/all_to_all | solution.py:51
  24.0 4.3 %copy-start.1 = (s32[16,1024]{1,0:T(8,128)S(1)}, s32[16,1024]{1,0:T(8,128)}, u32[]{:S(2)}) copy-start(s32[16,1024]{1,0:T(8,128)} %param.12) | copy-start | bytes 196612
  37.7 5.9 %copy-start.4 = (f32[1,16,1024]{2,1,0:T(8,128)S(1)}, f32[1,16,1024]{2,1,0:T(8,128)}, u32[]{:S(2)}) copy-start(f32[1,16,1024]{2,1,0:T(8,128)} %param.10) | copy-start | bytes 196612
  37.7 1.6 %collective-permute-start.2 = (f32[4,16,8,128]{3,0,2,1:T(4,128)S(1)}, f32[4,16,8,128]{3,0,2,1:T(4,128)S(1)}, u32[]{:S(2)}, u32[]{:S(2)}) collective-permute-start(f32[4,16,8,128]{3,0,2,1:T(4,128)S(1)} %all-to-all-done), channel_id=1, source_target_pairs={{0,16},{16,0},{1,17},{17,1},{2,18},{18,2},{3,19},{19,3},{4,20},{20... | collective-permute-start | bytes 786440 | tf_op jit(solution)/shard_map/ppermute | solution.py:34
  44.8 5.9 %collective-permute-start.3 = (f32[8,1,1024]{2,0,1:T(8,128)S(1)}, f32[8,1,1024]{2,0,1:T(8,128)S(1)}, u32[]{:S(2)}, u32[]{:S(2)}) collective-permute-start(f32[8,1,1024]{2,0,1:T(8,128)S(1)} %get-tuple-element.11), channel_id=1, source_target_pairs={{1,0},{2,1},{3,2},{4,3},{5,4},{6,5},{7,6},{8,7},{9,8},{10,9},{11,1... | collective-permute-start | bytes 98312 | tf_op jit(solution)/shard_map/ppermute | solution.py:20
  46.1 6.1 %collective-permute-start.4 = (f32[8,1,1024]{2,0,1:T(8,128)S(1)}, f32[8,1,1024]{2,0,1:T(8,128)S(1)}, u32[]{:S(2)}, u32[]{:S(2)}) collective-permute-start(f32[8,1,1024]{2,0,1:T(8,128)S(1)} %get-tuple-element.12), channel_id=1, source_target_pairs={{0,1},{1,2},{2,3},{3,4},{4,5},{5,6},{6,7},{7,8},{8,9},{9,10},{10,1... | collective-permute-start | bytes 98312 | tf_op jit(solution)/shard_map/ppermute | solution.py:18
  106.0 6.8 %copy-start.2 = (f32[12]{0:T(128)}, f32[12]{0:T(128)S(1)}, u32[]{:S(2)}) copy-start(f32[12]{0:T(128)S(1)} %get-tuple-element.6) | copy-start | bytes 148
where the time goes:
time: 114 us
  blocking collectives  44.3 us (39%)
  matrix products  25 us (22%)
  starting transfers between devices  20.9 us (18%)
  local copies, waits for them, and re-layouts  15.8 us (14%)
  waiting for transfers between devices  2.82 us (2%)
  between operations  2.77 us (2%)
  other arithmetic  2.05 us (2%)
    psum x1, blocking collectives, body(): lax.psum((local_dots, jnp.sum(vflat * vflat), local_gram), ('comp', 'tile'))  44.3 us
    ppermute x2, starting transfers between devices, extended(): lax.ppermute(tail, axis, [(i, (i + 1) % count) for i in range(ends)])  10 us
    dot_general x1, matrix products, body(): local_gram = jnp.dot(qmat, qmat.T, preferred_element_type=jnp.float32)  9.43 us
    all_to_all x1, starting transfers between devices, body(): lax.all_to_all(bucket, 'tile', split_axis=1, concat_axis=1, tiled=True)  8.18 us
    unnamed x14, local copies, waits for them, and re-layouts  8.08 us
    dot_general x1, matrix products, body(): jnp.dot(qmat, vflat, precision=lax.Precision.HIGHEST, preferred_element_t...  6.49 us
    dot_general x1, matrix products, body(): jnp.dot(coefs, qmat, precision=lax.Precision.HIGHEST, preferred_element_t...  4 us
    ppermute x2, starting transfers between devices, extended(): lax.ppermute(head, axis, [((i + 1) % count, i) for i in range(ends)])  2.58 us
  transfers between devices with their start and end apart: 6, of which 2 were waited for; matrix products, arithmetic and copies ran while one was open for 22% of the time, Pallas kernels for 0%

commit v1 on v0

--- a/solution.py
+++ b/solution.py
@@ -48,7 +48,9 @@
     nblk = rows * cols // 128
     surface = x[:FLUX].reshape(FLUX, nblk, 128)
     bucket = surface[:, send_rows[0, 0]]
-    moved = lax.all_to_all(bucket, "tile", split_axis=1, concat_axis=1, tiled=True)
+    parts = jnp.split(bucket, lax.axis_size("tile"), axis=1)
+    received = lax.all_to_all(jnp.stack(parts), "tile", 0, 0)
+    moved = jnp.concatenate(received, axis=1)
     arrived = from_partner(moved, "comp", 0)
     flat = arrived.reshape(FLUX, -1, 128)
     picked = flat[:, recv_slots[0, 0]]

time: 114 us -> 124 us (1.088)
  local copies, waits for them, and re-layouts: 15.8 us -> 25.1 us
    unnamed x14 -> x31, local copies, waits for them, and re-layouts: 8.08 us -> 17.2 us
  transfers between devices with their start and end apart: 6 -> 6, of which waited for: 2 -> 2; matrix products, arithmetic and copies ran while one was open for 22% -> 18% of each run, Pallas kernels for 0% -> 0%
where the time goes in v1:
time: 124 us; the launch traced here: 123 us
  blocking collectives  45.1 us (36%)
  local copies, waits for them, and re-layouts  25.1 us (20%)
  matrix products  25 us (20%)
  starting transfers between devices  20.9 us (17%)
  waiting for transfers between devices  2.97 us (2%)
  between operations  2.94 us (2%)
  other arithmetic  1.44 us (1%)
    psum x1, blocking collectives, body(): lax.psum((local_dots, jnp.sum(vflat * vflat), local_gram), ('comp', 'tile'))  45.1 us
    unnamed x31, local copies, waits for them, and re-layouts  17.2 us
    ppermute x2, starting transfers between devices, extended(): lax.ppermute(tail, axis, [(i, (i + 1) % count) for i in range(ends)])  9.91 us
    dot_general x1, matrix products, body(): local_gram = jnp.dot(qmat, qmat.T, preferred_element_type=jnp.float32)  9.43 us
    all_to_all x1, starting transfers between devices, body(): received = lax.all_to_all(jnp.stack(parts), 'tile', 0, 0)  8.34 us
    dot_general x1, matrix products, body(): jnp.dot(qmat, vflat, precision=lax.Precision.HIGHEST, preferred_element_t...  6.49 us
    dot_general x1, matrix products, body(): jnp.dot(coefs, qmat, precision=lax.Precision.HIGHEST, preferred_element_t...  4 us
    ppermute x2, starting transfers between devices, extended(): lax.ppermute(head, axis, [((i + 1) % count, i) for i in range(ends)])  2.58 us
  transfers between devices with their start and end apart: 6, of which 2 were waited for; matrix products, arithmetic and copies ran while one was open for 18% of the time, Pallas kernels for 0%

profile of v1, /device:TPU:0, one launch (start us, length us, event | category | flops | bytes accessed | tf_op | source)
XLA Modules:
  0.0 123.5 jit_solution(14271564420473378243)
XLA Ops:
  0.7 1.0 slice.68
  1.7 0.2 copy.74
  1.9 0.7 compare_select_fusion
  2.8 0.8 gather_fusion
  3.5 0.6 constant_dynamic-update-slice_fusion.15
  4.1 0.6 constant_dynamic-update-slice_fusion.14
  4.8 0.6 constant_dynamic-update-slice_fusion.13
  5.4 0.6 constant_dynamic-update-slice_fusion.12
  6.0 0.6 constant_dynamic-update-slice_fusion.11
  6.6 0.6 constant_dynamic-update-slice_fusion.10
  7.2 0.6 constant_dynamic-update-slice_fusion.9
  7.8 0.6 constant_dynamic-update-slice_fusion.8
  8.4 0.6 constant_dynamic-update-slice_fusion.7
  9.0 0.6 constant_dynamic-update-slice_fusion.6
  9.6 0.6 constant_dynamic-update-slice_fusion.5
  10.2 0.6 constant_dynamic-update-slice_fusion.4
  10.8 0.6 constant_dynamic-update-slice_fusion.3
  11.4 0.6 constant_dynamic-update-slice_fusion.2
  12.0 0.6 constant_dynamic-update-slice_fusion.1
  12.6 0.6 constant_dynamic-update-slice_fusion
  13.3 8.3 %all-to-all-start = ((f32[16,4,1,8,128]{4,3,1,2,0:T(8,128)}), f32[16,4,1,8,128]{4,3,1,2,0:T(8,128)S(1)}, u32[]{:S(2)}, u32[]{:S(2)}) async-start(f32[16,4,1,8,128]{4,3,1,2,0:T(8,128)} %constant_dynamic-update-slice_fusion), calls=%async_computation | async-start | bytes 524288 | tf_op jit(solution)/shard_map/all_to_all | solution.py:52
  21.6 1.4 %copy.99 = f32[1,8,16,1024]{3,1,2,0:T(8,128)S(1)} copy(f32[1,8,16,1024]{3,2,1,0:T(8,128)} %param.8) | data formatting | bytes 1048576 | tf_op args[0]
  23.0 1.3 %collective-permute-start = (f32[8,1,1024]{2,0,1:T(8,128)S(1)}, f32[8,1,1024]{2,0,1:T(8,128)S(1)}, u32[]{:S(2)}, u32[]{:S(2)}) collective-permute-start(f32[8,1,1024]{2,0,1:T(8,128)S(1)} %get-tuple-element.17), channel_id=1, source_target_pairs={{1,0},{2,1},{3,2},{4,3},{5,4},{6,5},{7,6},{8,7},{9,8},{10,9},{11,1... | collective-permute-start | bytes 98312 | tf_op jit(solution)/shard_map/ppermute | solution.py:20
  24.3 4.5 %collective-permute-start.1 = (f32[8,1,1024]{2,0,1:T(8,128)S(1)}, f32[8,1,1024]{2,0,1:T(8,128)S(1)}, u32[]{:S(2)}, u32[]{:S(2)}) collective-permute-start(f32[8,1,1024]{2,0,1:T(8,128)S(1)} %get-tuple-element.18), channel_id=1, source_target_pairs={{0,1},{1,2},{2,3},{3,4},{4,5},{5,6},{6,7},{7,8},{8,9},{9,10},{10,1... | collective-permute-start | bytes 98312 | tf_op jit(solution)/shard_map/ppermute | solution.py:18
  28.9 0.1 copy.77
  29.2 0.1 copy.83
  29.3 2.3 %pad.27 = bf16[16,128,1024]{2,1,0:T(8,128)(2,1)S(1)} pad(bf16[12,128,1024]{2,1,0:T(8,128)(2,1)} %bitcast.158, bf16[]{:T(256)} %constant.69), padding=0_4x0_0x0_0 | pad | bytes 7340034
  31.6 4.3 %copy.89 = bf16[2,8,128,1024]{3,1,2,0:T(8,128)(2,1)} copy(bf16[2,8,128,1024]{3,2,1,0:T(8,128)(2,1)S(1)} %bitcast.151) | data formatting | bytes 8388608
  35.9 9.4 %fusion.7 = f32[12,12]{1,0:T(8,128)S(1)} fusion(bf16[12,8,16,1024]{3,2,1,0:T(8,128)(2,1)} %bitcast.159), kind=kOutput, calls=%fused_computation.11 | convolution fusion | flops 37748736 | bytes 3146304 | tf_op jit(solution)/shard_map/dot_general | solution.py:71
  45.5 0.2 fusion.34
  45.7 1.3 %collective-permute-done.2 = f32[4,16,8,128]{3,2,1,0:T(8,128)S(1)} collective-permute-done((f32[4,16,8,128]{3,2,1,0:T(8,128)S(1)}, f32[4,16,8,128]{3,2,1,0:T(8,128)S(1)}, u32[]{:S(2)}, u32[]{:S(2)}) %collective-permute-start.2) | collective-permute-done | bytes 262176 | tf_op jit(solution)/shard_map/ppermute | solution.py:34
  47.0 0.2 copy.78
  47.2 2.3 %gather_fusion.1 = f32[512,4,128]{2,1,0:T(4,128)S(1)} fusion(f32[4,128,128]{2,0,1:T(4,128)S(1)} %copy.78, s32[1024]{0:T(1024)S(1)} %pad_clamp_fusion), kind=kCustom, calls=%fused_computation.1 | custom fusion | bytes 2099200 | tf_op jit(solution)/shard_map/gather | solution.py:56
  49.4 2.0 %fusion.11 = f32[128,1,4,128]{3,1,2,0:T(1,128)S(1)} fusion(f32[128,4,1,1]{1,2,3,0:T(1,128)S(1)} %copy.83, f32[4,128,4,128]{3,0,2,1:T(4,128)S(1)} %bitcast.157), kind=kOutput, calls=%fused_computation.15 | convolution fusion | flops 3145728 | bytes 1312768 | tf_op jit(solution)/shard_map/ek,fekq->feq/dot_general | solution.py:57
  51.5 0.9 fusion.6
  52.4 0.2 fusion.31
  52.6 1.3 %collective-permute-start.3 = (f32[8,1,1024]{2,0,1:T(8,128)S(1)}, f32[8,1,1024]{2,0,1:T(8,128)S(1)}, u32[]{:S(2)}, u32[]{:S(2)}) collective-permute-start(f32[8,1,1024]{2,0,1:T(8,128)S(1)} %get-tuple-element.11), channel_id=1, source_target_pairs={{1,0},{2,1},{3,2},{4,3},{5,4},{6,5},{7,6},{8,7},{9,8},{10,9},{11,1... | collective-permute-start | bytes 98312 | tf_op jit(solution)/shard_map/ppermute | solution.py:20
  53.9 5.4 %collective-permute-start.4 = (f32[8,1,1024]{2,0,1:T(8,128)S(1)}, f32[8,1,1024]{2,0,1:T(8,128)S(1)}, u32[]{:S(2)}, u32[]{:S(2)}) collective-permute-start(f32[8,1,1024]{2,0,1:T(8,128)S(1)} %get-tuple-element.12), channel_id=1, source_target_pairs={{0,1},{1,2},{2,3},{3,4},{4,5},{5,6},{6,7},{7,8},{8,9},{9,10},{10,1... | collective-permute-start | bytes 98312 | tf_op jit(solution)/shard_map/ppermute | solution.py:18
  59.3 1.6 %collective-permute-done.4 = f32[8,1,1024]{2,0,1:T(8,128)S(1)} collective-permute-done((f32[8,1,1024]{2,0,1:T(8,128)S(1)}, f32[8,1,1024]{2,0,1:T(8,128)S(1)}, u32[]{:S(2)}, u32[]{:S(2)}) %collective-permute-start.4) | collective-permute-done | bytes 32800 | tf_op jit(solution)/shard_map/ppermute | solution.py:18
  61.0 1.4 %multiply_reduce_fusion = (f32[]{:T(128)}, f32[8,16,1024]{2,0,1:T(8,128)S(1)}) fusion(f32[4,16,1024]{2,0,1:T(4,128)S(1)} %bitcast.182, f32[8,16,1024]{2,0,1:T(8,128)S(1)} %fusion.6, f32[1,8,8]{2,1,0:T(8,128)S(1)} %copy-done, f32[8,16,1]{2,0,1:T(8,128)S(1)} %get-tuple-element.9, f32[8,16,1023]{2,0,1:T(8,128)S(1)} %get-tuple-element.7, ...), kind=kOutput, calls=%fused_computation.35 | convolution fusion | flops 14680063 | bytes 2556164 | tf_op jit(solution)/shard_map/lm,mrq->lrq/dot_general | solution.py:40
  62.4 0.3 copy.79
  62.7 0.6 reshape.117
  63.4 6.5 %convolution_bitcast_fusion.1 = f32[12]{0:T(128)S(1)} fusion(f32[131072,1]{0,1:T(1,128)S(1)} %reshape.117, bf16[12,131072]{1,0:T(8,128)(2,1)} %bitcast.149), kind=kOutput, calls=%fused_computation.12 | convolution fusion | flops 18874368 | bytes 3670064 | tf_op jit(solution)/shard_map/dot_general | solution.py:68
  69.9 45.1 %all-reduce.1 = (f32[12]{0:T(128)S(1)}, f32[]{:T(128)}, f32[12,12]{1,0:T(8,128)S(1)}) all-reduce(f32[12]{0:T(128)S(1)} %convolution_bitcast_fusion.1, f32[]{:T(128)} %get-tuple-element.19, f32[12,12]{1,0:T(8,128)S(1)} %fusion.7), channel_id=1, replica_groups=mesh['comp'=2,'tile'=16] {'comp','tile'}, use_global_device_ids=true, to_apply=%region_0.1 | all-reduce | flops 157 | bytes 1256 | tf_op jit(solution)/shard_map/psum | solution.py:72
  115.0 0.7 multiply_reduce_fusion.1
  115.7 4.0 %fusion.29 = f32[1,131072]{1,0:T(1,128)S(1)} fusion(bf16[12,131072]{1,0:T(8,128)(2,1)} %bitcast.150, f32[12]{0:T(128)S(1)} %get-tuple-element.6), kind=kOutput, calls=%fused_computation.79 | convolution fusion | flops 18874368 | bytes 3670064 | tf_op jit(solution)/shard_map/dot_general | solution.py:76
  119.7 0.8 fusion.13
  122.6 0.9 reshape.95
  (33 shorter events, 0.8 us)
Async XLA Ops:
  0.6 50.8 %copy-start = (f32[1,8,8]{2,1,0:T(8,128)S(1)}, f32[1,8,8]{2,1,0:T(8,128)}, u32[]{:S(2)}) copy-start(f32[1,8,8]{2,1,0:T(8,128)} %param.11) | copy-start | bytes 772
  0.6 28.3 %copy-start.4 = (s32[1,1,128,4]{2,3,1,0:T(4,128)S(1)}, s32[1,1,128,4]{2,3,1,0:T(4,128)}, u32[]{:S(2)}) copy-start(s32[1,1,128,4]{2,3,1,0:T(4,128)} %param.14) | copy-start | bytes 6148
  0.7 28.5 %copy-start.3 = (f32[1,1,128,4]{2,3,1,0:T(4,128)S(1)}, f32[1,1,128,4]{2,3,1,0:T(4,128)}, u32[]{:S(2)}) copy-start(f32[1,1,128,4]{2,3,1,0:T(4,128)} %param.15) | copy-start | bytes 6148
  13.3 32.1 %all-to-all-start = ((f32[16,4,1,8,128]{4,3,1,2,0:T(8,128)}), f32[16,4,1,8,128]{4,3,1,2,0:T(8,128)S(1)}, u32[]{:S(2)}, u32[]{:S(2)}) async-start(f32[16,4,1,8,128]{4,3,1,2,0:T(8,128)} %constant_dynamic-update-slice_fusion), calls=%async_computation | async-start | bytes 524288 | tf_op jit(solution)/shard_map/all_to_all | solution.py:52
  23.0 28.5 %collective-permute-start = (f32[8,1,1024]{2,0,1:T(8,128)S(1)}, f32[8,1,1024]{2,0,1:T(8,128)S(1)}, u32[]{:S(2)}, u32[]{:S(2)}) collective-permute-start(f32[8,1,1024]{2,0,1:T(8,128)S(1)} %get-tuple-element.17), channel_id=1, source_target_pairs={{1,0},{2,1},{3,2},{4,3},{5,4},{6,5},{7,6},{8,7},{9,8},{10,9},{11,1... | collective-permute-start | bytes 98312 | tf_op jit(solution)/shard_map/ppermute | solution.py:20
  24.3 27.2 %collective-permute-start.1 = (f32[8,1,1024]{2,0,1:T(8,128)S(1)}, f32[8,1,1024]{2,0,1:T(8,128)S(1)}, u32[]{:S(2)}, u32[]{:S(2)}) collective-permute-start(f32[8,1,1024]{2,0,1:T(8,128)S(1)} %get-tuple-element.18), channel_id=1, source_target_pairs={{0,1},{1,2},{2,3},{3,4},{4,5},{5,6},{6,7},{7,8},{8,9},{9,10},{10,1... | collective-permute-start | bytes 98312 | tf_op jit(solution)/shard_map/ppermute | solution.py:18
  31.6 4.3 %copy-start.1 = (s32[16,1024]{1,0:T(8,128)S(1)}, s32[16,1024]{1,0:T(8,128)}, u32[]{:S(2)}) copy-start(s32[16,1024]{1,0:T(8,128)} %param.12) | copy-start | bytes 196612
  45.3 6.1 %copy-start.5 = (f32[1,16,1024]{2,1,0:T(8,128)S(1)}, f32[1,16,1024]{2,1,0:T(8,128)}, u32[]{:S(2)}) copy-start(f32[1,16,1024]{2,1,0:T(8,128)} %param.10) | copy-start | bytes 196612
  45.4 1.6 %collective-permute-start.2 = (f32[4,16,8,128]{3,2,1,0:T(8,128)S(1)}, f32[4,16,8,128]{3,2,1,0:T(8,128)S(1)}, u32[]{:S(2)}, u32[]{:S(2)}) collective-permute-start(f32[4,16,8,128]{3,2,1,0:T(8,128)S(1)} %bitcast.179), channel_id=1, source_target_pairs={{0,16},{16,0},{1,17},{17,1},{2,18},{18,2},{3,19},{19,3},{4,20},{20... | collective-permute-start | bytes 786440 | tf_op jit(solution)/shard_map/ppermute | solution.py:34
  52.6 6.8 %collective-permute-start.3 = (f32[8,1,1024]{2,0,1:T(8,128)S(1)}, f32[8,1,1024]{2,0,1:T(8,128)S(1)}, u32[]{:S(2)}, u32[]{:S(2)}) collective-permute-start(f32[8,1,1024]{2,0,1:T(8,128)S(1)} %get-tuple-element.11), channel_id=1, source_target_pairs={{1,0},{2,1},{3,2},{4,3},{5,4},{6,5},{7,6},{8,7},{9,8},{10,9},{11,1... | collective-permute-start | bytes 98312 | tf_op jit(solution)/shard_map/ppermute | solution.py:20
  53.9 7.1 %collective-permute-start.4 = (f32[8,1,1024]{2,0,1:T(8,128)S(1)}, f32[8,1,1024]{2,0,1:T(8,128)S(1)}, u32[]{:S(2)}, u32[]{:S(2)}) collective-permute-start(f32[8,1,1024]{2,0,1:T(8,128)S(1)} %get-tuple-element.12), channel_id=1, source_target_pairs={{0,1},{1,2},{2,3},{3,4},{4,5},{5,6},{6,7},{7,8},{8,9},{9,10},{10,1... | collective-permute-start | bytes 98312 | tf_op jit(solution)/shard_map/ppermute | solution.py:18
  115.7 6.9 %copy-start.2 = (f32[12]{0:T(128)}, f32[12]{0:T(128)S(1)}, u32[]{:S(2)}) copy-start(f32[12]{0:T(128)S(1)} %get-tuple-element.6) | copy-start | bytes 148
